TPU v7x, 32 devices: a whole 2x2x4 slice. The times are simulated.
32 devices in a mesh: req: 8 (over z, x), tp: 4 (over y, core).
Axes of the slice: x: 2, y: 2, z: 4, core: 2. Of those that a mesh axis runs over, the one named last changes fastest.
Arguments:
- hidden_in: bfloat16 [8, 1024, 2048], P('req', None, 'tp'), may hold values from -6 to 6
- ln_gain: float32 [2048], replicated, may hold values from 0.25 to 1.75
- ln_bias: float32 [2048], replicated, may hold values from -1.5 to 1.5
- w_qkv: bfloat16 [3, 2048, 2048], P(None, None, 'tp'), may hold values from -0.125 to 0.125
- b_qkv: float32 [3, 2048], P(None, 'tp'), may hold values from -1.5 to 1.5
- w_out: bfloat16 [2048, 2048], P('tp'), may hold values from -0.125 to 0.125
- b_out: float32 [2048], replicated, may hold values from -1.5 to 1.5
- alibi_slope: float32 [16], P('tp'), may hold values from 2.4414063e-05 to 0.1
- prefix_k: bfloat16 [2048, 2048], P('req', 'tp'), may hold values from -160 to 160
- prefix_v: bfloat16 [2048, 2048], P('req', 'tp'), may hold values from -6 to 6
- suffix_len: int32 [8], P('req'), may hold values from 64 to 1024, as said below
- group_of: int32 [8], P('req'), may hold values from 0 to 1
- block_of_device: int32 [8], P('req'), may hold values from 0 to 7, each once
Outputs:
- mixed: bfloat16 [8, 1024, 2048], P('req', None, 'tp')
- cache_k: bfloat16 [8, 1024, 2048], P('req', None, 'tp')
- cache_v: bfloat16 [8, 1024, 2048], P('req', None, 'tp')
Inputs may be any that keep to these rules, and one draw needn't show every extreme that they name: `suffix_len`: every request has at least 64 live slots; some request has exactly 1024.
All inputs are finite; a program needn't handle non-finite values.
Results may differ from a plain program's by a relative error of at most 0.011.
Values may be sent and summed in bfloat16 or wider, within the bound.
A program may use at most 384 MiB of HBM per device.

v0:
```python
import jax
import jax.numpy as jnp
from jax import lax
from jax.sharding import PartitionSpec as P

EPS = 1e-05
NEGATIVE = -1e30


def on_device(
    hidden_in,
    ln_gain,
    ln_bias,
    w_qkv,
    b_qkv,
    w_out,
    b_out,
    alibi_slope,
    prefix_k,
    prefix_v,
    suffix_len,
    group_of,
    block_of_device,
):
    local_rows = hidden_in[0]
    slots = local_rows.shape[0]
    width_dev = local_rows.shape[1]
    gathered = lax.all_gather(local_rows, "tp", axis=1, tiled=True)
    values32 = gathered.astype(jnp.float32)
    center = values32 - jnp.mean(values32, axis=1, keepdims=True)
    spread = jnp.mean(center * center, axis=1, keepdims=True)
    normed = (center / jnp.sqrt(spread + EPS) * ln_gain + ln_bias).astype(jnp.bfloat16)
    projected = (
        jnp.einsum("sd,cdh->csh", normed, w_qkv, preferred_element_type=jnp.float32)
        + b_qkv[:, None, :]
    )
    projected = projected.astype(jnp.bfloat16)
    query, keys, values = (projected[0], projected[1], projected[2])
    length = suffix_len[0]
    my_group = group_of[0]
    slot_ids = lax.iota(jnp.int32, slots)
    live = slot_ids < length
    keys_out = jnp.where(live[:, None], keys, jnp.zeros_like(keys))
    values_out = jnp.where(live[:, None], values, jnp.zeros_like(values))
    heads_dev = alibi_slope.shape[0]
    head_size = query.shape[1] // heads_dev
    attn_scale = 1.0 / jnp.sqrt(jnp.float32(head_size))
    query_heads = query.reshape(slots, heads_dev, head_size)
    block_tokens = prefix_k.shape[0]
    half_count = lax.axis_size("req") // 2
    prefix_total = half_count * block_tokens
    block_numbers = jnp.full((block_tokens,), block_of_device[0], jnp.int32)
    query_pos = (prefix_total + slot_ids).astype(jnp.float32)
    key_piece = lax.all_gather(prefix_k, "req", axis=0, tiled=True)
    value_piece = lax.all_gather(prefix_v, "req", axis=0, tiled=True)
    number_piece = lax.all_gather(block_numbers, "req", axis=0, tiled=True)
    count = key_piece.shape[0]
    offsets = lax.iota(jnp.int32, count) % block_tokens
    key_pos = (number_piece % half_count * block_tokens + offsets).astype(jnp.float32)
    fold_allowed = number_piece // half_count == my_group
    compute_old_max = jnp.full((heads_dev, slots), NEGATIVE, jnp.float32)
    compute_key_heads = key_piece.reshape(count, heads_dev, head_size)
    compute_value_heads = value_piece.reshape(count, heads_dev, head_size)
    compute_scores = (
        jnp.einsum(
            "shd,khd->hsk", query_heads, compute_key_heads, preferred_element_type=jnp.float32
        )
        * attn_scale
    )
    compute_scores = compute_scores - alibi_slope[:, None, None] * (
        query_pos[None, :, None] - key_pos[None, None, :]
    )
    compute_scores = jnp.where(fold_allowed[None, None, :], compute_scores, NEGATIVE)
    compute_new_max = jnp.maximum(compute_old_max, jnp.max(compute_scores, axis=2))
    compute_weights = jnp.where(
        fold_allowed[None, None, :], jnp.exp(compute_scores - compute_new_max[:, :, None]), 0.0
    )
    compute_new_sum = jnp.sum(compute_weights, axis=2)
    compute_new_acc = jnp.einsum(
        "hsk,khd->hsd",
        compute_weights.astype(jnp.bfloat16),
        compute_value_heads,
        preferred_element_type=jnp.float32,
    )
    key_heads = keys.reshape(slots, heads_dev, head_size)
    value_heads = values.reshape(slots, heads_dev, head_size)
    row_block = min(512, slots)
    pieces_out = []
    for row_start in range(0, slots, row_block):
        row_stop = min(slots, row_start + row_block)
        row_ids = slot_ids[row_start:row_stop]
        query_block = query_heads[row_start:row_stop]
        scores = (
            jnp.einsum("shd,khd->hsk", query_block, key_heads, preferred_element_type=jnp.float32)
            * attn_scale
        )
        scores = (
            scores
            - alibi_slope[:, None, None]
            * (row_ids[:, None] - slot_ids[None, :]).astype(jnp.float32)[None]
        )
        allowed = (slot_ids[None, :] <= row_ids[:, None]) & (slot_ids[None, :] < length)
        scores = jnp.where(allowed[None], scores, NEGATIVE)
        old_max = compute_new_max[:, row_start:row_stop]
        new_max = jnp.maximum(old_max, jnp.max(scores, axis=2))
        weights = jnp.where(allowed[None], jnp.exp(scores - new_max[:, :, None]), 0.0)
        factor = jnp.exp(old_max - new_max)
        new_sum = compute_new_sum[:, row_start:row_stop] * factor + jnp.sum(weights, axis=2)
        new_acc = compute_new_acc[:, row_start:row_stop] * factor[:, :, None] + jnp.einsum(
            "hsk,khd->hsd",
            weights.astype(jnp.bfloat16),
            value_heads,
            preferred_element_type=jnp.float32,
        )
        piece_out = new_acc / new_sum[:, :, None]
        pieces_out.append(piece_out)
    attended = jnp.concatenate(pieces_out, axis=1)
    attended = (
        attended.transpose(1, 0, 2).reshape(slots, heads_dev * head_size).astype(jnp.bfloat16)
    )
    partial_value = jnp.dot(attended, w_out, preferred_element_type=jnp.float32)
    summed = lax.psum_scatter(
        partial_value.astype(jnp.bfloat16), "tp", scatter_dimension=1, tiled=True
    ).astype(jnp.float32)
    bias_part = lax.dynamic_slice_in_dim(b_out, lax.axis_index("tp") * width_dev, width_dev)
    result = summed + bias_part + local_rows.astype(jnp.float32)
    result = jnp.where(live[:, None], result, 0.0).astype(jnp.bfloat16)
    return (result[None], keys_out[None], values_out[None])


def solution(mesh):
    return jax.shard_map(
        on_device,
        mesh=mesh,
        in_specs=(
            P("req", None, "tp"),
            P(),
            P(),
            P(None, None, "tp"),
            P(None, "tp"),
            P("tp", None),
            P(),
            P("tp"),
            P("req", "tp"),
            P("req", "tp"),
            P("req"),
            P("req"),
            P("req"),
        ),
        out_specs=(P("req", None, "tp"), P("req", None, "tp"), P("req", None, "tp")),
        check_vma=False,
    )
```

profile of v0, /device:TPU:0, one launch (start us, length us, event | category | flops | bytes accessed | tf_op | source)
XLA Modules:
  0.0 241.2 jit_solution(5262396388451075236)
XLA Ops:
  7.2 0.0 copy-start
  7.2 0.0 all-gather.10.cloned.1.call-start
  7.2 0.7 all-gather.10.cloned.1.call-update
  7.9 0.0 all-gather.6.cloned.1.call-start
  8.0 1.8 copy.42
  9.8 0.0 all-gather.6.cloned.1.call-update
  9.8 0.0 all-gather.8.cloned.1.call-start
  9.8 1.8 copy.45
  11.6 0.0 all-gather.8.cloned.1.call-update
  11.6 0.0 reduce-scatter.2.cloned.1.call-start
  12.4 2.4 subtract_convert_fusion
  14.8 1.8 fusion.35
  17.2 22.2 %all-gather.1 = s32[8,1,256]{2,1,0:T(1,128)S(1)} all-gather(s32[1,1,256]{2,1,0:T(1,128)S(1)} %broadcast.168), channel_id=1, replica_groups=mesh['req'=8,'tp'=4] {'req'}, dimensions={0}, use_global_device_ids=true | all-gather | bytes 9216 | tf_op jit(solution)/shard_map/all_gather | solution.py:56
  40.2 0.0 copy-start.15
  40.2 0.0 copy-start.16
  40.2 0.0 copy-start.17
  40.2 3.8 %broadcast_subtract_fusion = f32[1024,2048]{1,0:T(8,128)} fusion(f32[2048]{0:T(1024)S(1)} %fusion.50, f32[1024]{0:T(1024)S(1)} %add_convert_fusion.1), kind=kLoop, calls=%fused_computation.28 | loop fusion | flops 2097152 | bytes 8400896 | tf_op jit(solution)/shard_map/sub | solution.py:71
  44.0 2.8 %all-gather.10.cloned.1.call-done = bf16[1,1024,2048]{2,1,0:T(8,128)(2,1)} async-done(((bf16[1,1024,512]{2,1,0:T(8,128)(2,1)}), bf16[1,1024,2048]{2,1,0:T(8,128)(2,1)}) %all-gather.10.cloned.1.call-update) | async-done | bytes 4194320 | tf_op jit(solution)/shard_map/all_gather | solution.py:28
  46.8 3.0 %convert_reduce_fusion = f32[1024]{0:T(1024)S(1)} fusion(bf16[1,1024,2048]{2,1,0:T(8,128)(2,1)} %all-gather.10.cloned.1.call-done), kind=kLoop, calls=%fused_computation.6 | loop fusion | flops 4193280 | bytes 4198400 | tf_op jit(solution)/shard_map/reduce_sum | solution.py:30
  49.8 3.4 %fusion.8 = f32[1024]{0:T(1024)S(1)} fusion(bf16[1,1024,2048]{2,1,0:T(8,128)(2,1)} %all-gather.10.cloned.1.call-done, f32[1024]{0:T(1024)S(1)} %broadcast_multiply_fusion), kind=kLoop, calls=%fused_computation.11 | loop fusion | flops 8387584 | bytes 4202496 | tf_op jit(solution)/shard_map/reduce_sum | solution.py:31
  53.2 0.0 copy-done.15
  53.2 0.0 copy-done.16
  53.2 0.0 copy-done.17
  53.2 0.0 copy-done.1
  53.2 11.3 %fusion.29 = bf16[3,1024,512]{1,2,0:T(8,128)(2,1)S(1)} fusion(f32[3,512]{1,0:T(4,128)S(1)} %copy-done.15, bf16[3,2048,512]{2,1,0:T(8,128)(2,1)} %param.16, bf16[1,1024,2048]{2,1,0:T(8,128)(2,1)S(1)} %copy-done.1, f32[2048]{0:T(1024)S(1)} %copy-done.16, f32[2048]{0:T(1024)S(1)} %copy-done.17, f32[1024]{0:T(1024)S(1)} %add_sqrt_fusion, ...), kind=kOutput, calls=%fused_computation.36 | convolution fusion | flops 6458179584 | bytes 13662208 | tf_op jit(solution)/shard_map/sd,cdh->csh/dot_general | solution.py:34
  64.5 0.0 copy-start.14
  64.5 2.1 broadcast_select_fusion
  66.7 1.1 fusion.65
  67.7 32.2 %all-gather.6.cloned.1.call-done = bf16[2048,512]{0,1:T(8,128)(2,1)} async-done(((bf16[256,512]{0,1:T(8,128)(2,1)}), bf16[2048,512]{0,1:T(8,128)(2,1)}) %all-gather.6.cloned.1.call-update) | async-done | bytes 2097168 | tf_op jit(solution)/shard_map/all_gather | solution.py:54
  99.9 0.0 copy-done.14
  99.9 17.8 %fusion.66 = (f32[4,1024]{1,0:T(4,128)S(1)}, f32[4,1024,2048]{2,1,0:T(8,128)}) fusion(f32[1024,2048]{1,0:T(8,128)} %broadcast_subtract_fusion, f32[4]{0:T(128)S(1)} %copy-done.14, bf16[1024,4,128]{0,2,1:T(8,128)(2,1)S(1)} %bitcast.62, bf16[2048,4,128]{0,2,1:T(8,128)(2,1)} %bitcast.63, pred[2048]{0:T(1024)(128)(4,1)S(1)} %fusion.47), kind=kOutput, calls=%fused_computation.94 | convolution fusion | flops 2189422592 | bytes 45107216 | tf_op jit(solution)/shard_map/shd,khd->hsk/dot_general | solution.py:65
  117.8 0.0 copy-start.7
  117.8 0.0 copy-start.10
  117.8 0.0 copy-start.11
  117.8 0.0 copy-start.13
  117.8 4.5 %fusion.16 = (f32[4,512]{1,0:T(4,128)S(1)}, f32[4,512,1024]{2,1,0:T(8,128)S(1)}) fusion(f32[512,1024]{1,0:T(8,128)} %get-tuple-element.35, f32[4]{0:T(128)S(1)} %copy-done.14, pred[512,1024]{1,0:T(8,128)(4,1)} %get-tuple-element.28, bf16[512,4,128]{0,2,1:T(8,128)(2,1)} %bitcast.70, bf16[1024,4,128]{0,2,1:T(8,128)(2,1)} %bitcast.66), kind=kOutput, calls=%fused_computation.24 | convolution fusion | flops 547354624 | bytes 12591120 | tf_op jit(solution)/shard_map/shd,khd->hsk/dot_general | solution.py:94
  122.4 0.0 copy-start.18
  122.4 0.0 copy-done.3
  122.4 0.0 copy-done.6
  122.4 0.0 copy-done.7
  122.4 0.0 copy-done.10
  122.4 0.0 copy-done.11
  122.4 0.0 copy-done.13
  122.4 7.8 %fusion.12 = (f32[4,512]{1,0:T(4,128)S(1)}, f32[4,512]{1,0:T(4,128)S(1)}, f32[4,512,1024]{2,1,0:T(8,128)}) fusion(f32[4,512,1024]{2,1,0:T(8,128)S(1)} %get-tuple-element.30, f32[4,512]{1,0:T(4,128)S(1)} %slice_maximum_fusion.1, f32[512,1024]{1,0:T(8,128)S(1)} %copy-done.7, f32[4]{0:T(128)S(1)} %copy-done.14, pred[512,1024]{1,0:T(8,128)(4,1)S(1)} %copy-done.11, ...), kind=kOutput, calls=%fused_computation.19 | convolution fusion | flops 562032640 | bytes 23617552 | tf_op jit(solution)/shard_map/shd,khd->hsk/dot_general | solution.py:94
  130.2 0.0 copy-done.18
  130.2 14.3 %fusion = f32[4,1024]{1,0:T(4,128)S(1)} fusion(f32[4,1024,2048]{2,1,0:T(8,128)} %get-tuple-element.32, f32[4,1024]{1,0:T(4,128)S(1)} %broadcast_maximum_fusion, pred[2048]{0:T(1024)(128)(4,1)S(1)} %fusion.47), kind=kLoop, calls=%fused_computation.2 | loop fusion | flops 25161728 | bytes 33589248 | tf_op jit(solution)/shard_map/reduce_sum | solution.py:78
  144.6 6.7 %all-gather.8.cloned.1.call-done = bf16[2048,512]{0,1:T(8,128)(2,1)} async-done(((bf16[256,512]{0,1:T(8,128)(2,1)}), bf16[2048,512]{0,1:T(8,128)(2,1)}) %all-gather.8.cloned.1.call-update) | async-done | bytes 2097168 | tf_op jit(solution)/shard_map/all_gather | solution.py:55
  151.3 15.1 %fusion.2 = f32[4,1024,128]{2,1,0:T(8,128)} fusion(bf16[2048,4,128]{0,2,1:T(8,128)(2,1)} %bitcast.73, f32[4,1024,2048]{2,1,0:T(8,128)} %get-tuple-element.32, f32[4,1024]{1,0:T(4,128)S(1)} %broadcast_maximum_fusion, pred[2048]{0:T(1024)(128)(4,1)S(1)} %fusion.47), kind=kOutput, calls=%fused_computation.4 | convolution fusion | flops 2172649472 | bytes 37767168 | tf_op jit(solution)/shard_map/hsk,khd->hsd/dot_general | solution.py:79
  166.4 0.0 copy-done.4
  166.4 0.0 slice-start
  166.4 6.0 %fusion.14 = f32[4,512]{1,0:T(4,128)S(1)} fusion(f32[4,512,1024]{2,1,0:T(8,128)} %get-tuple-element.33, f32[4,512]{1,0:T(4,128)S(1)} %slice_maximum_fusion, f32[512,1024]{1,0:T(8,128)S(1)} %copy-done.4, f32[4]{0:T(128)S(1)} %copy-done.14, pred[512,1024]{1,0:T(8,128)(4,1)S(1)} %copy-done.6), kind=kLoop, calls=%fused_computation.21 | loop fusion | flops 14678016 | bytes 11026448 | tf_op jit(solution)/shard_map/reduce_sum | solution.py:108
  172.4 0.0 copy-done.2
  172.5 0.0 slice-start.1
  172.5 5.8 %divide_convert_fusion = bf16[4,512,128]{2,1,0:T(8,128)(2,1)S(1)} fusion(bf16[1024,4,128]{0,2,1:T(8,128)(2,1)S(1)} %bitcast.64, f32[4,512,1024]{2,1,0:T(8,128)S(1)} %copy-done.2, f32[4,512]{1,0:T(4,128)S(1)} %slice_maximum_fusion, f32[512,1024]{1,0:T(8,128)S(1)} %copy-done.4, f32[4]{0:T(128)S(1)} %copy-done.14, pred[512,1024]{1,0:T(8,128)(4,1)S(1)} %copy-done.6, ...), kind=kOutput, calls=%fused_computation.52 | convolution fusion | flops 552599552 | bytes 13656080 | tf_op jit(solution)/shard_map/hsk,khd->hsd/dot_general | solution.py:109
  178.4 3.8 %divide_convert_fusion.1 = bf16[4,512,128]{2,1,0:T(8,128)(2,1)S(1)} fusion(bf16[1024,4,128]{0,2,1:T(8,128)(2,1)S(1)} %bitcast.65, f32[4,512,1024]{2,1,0:T(8,128)S(1)} %bitcast.75, f32[4,512]{1,0:T(4,128)S(1)} %slice_maximum_fusion.1, f32[512,1024]{1,0:T(8,128)S(1)} %copy-done.8, f32[4]{0:T(128)S(1)} %copy-done.14, pred[512,1024]{1,0:T(8,128)(4,1)S(1)} %copy-done.12, ...), kind=kOutput, calls=%fused_computation.53 | convolution fusion | flops 552599552 | bytes 13656080 | tf_op jit(solution)/shard_map/hsk,khd->hsd/dot_general | solution.py:109
  182.1 0.1 maximum_bitcast_fusion
  182.2 1.3 copy.53
  183.5 5.7 %convolution_convert_fusion = bf16[1024,2048]{1,0:T(8,128)(2,1)} fusion(bf16[1024,512]{0,1:T(8,128)(2,1)} %bitcast.68, bf16[512,2048]{1,0:T(8,128)(2,1)S(1)} %copy-done), kind=kOutput, calls=%fused_computation.35 | convolution fusion | flops 2149580800 | bytes 7340032 | tf_op jit(solution)/shard_map/dot_general | solution.py:121
  189.2 0.0 reduce-scatter.2.cloned.1.call-update
  189.2 0.8 dynamic_slice.3
  190.0 2.3 copy.54
  192.3 2.5 %copy.55 = bf16[1,1024,512]{2,1,0:T(8,128)(2,1)} copy(bf16[1,1024,512]{1,2,0:T(8,128)(2,1)} %get-tuple-element.18) | data formatting | bytes 2097152
  194.8 37.3 %reduce-scatter.2.cloned.1.call-done = bf16[1024,512]{1,0:T(8,128)(2,1)} async-done(((bf16[1024,2048]{1,0:T(8,128)(2,1)}), bf16[1024,512]{1,0:T(8,128)(2,1)}) %reduce-scatter.2.cloned.1.call-update) | async-done | bytes 1048592 | tf_op jit(solution)/shard_map/reduce_scatter | solution.py:122
  232.1 2.6 %fusion.42 = bf16[1,1024,512]{2,1,0:T(8,128)(2,1)} fusion(bf16[1024,512]{1,0:T(8,128)(2,1)} %reduce-scatter.2.cloned.1.call-done, bf16[1,1024,512]{2,1,0:T(8,128)(2,1)S(1)} %copy-done.5, f32[512]{0:T(512)S(1)} %dynamic_slice.3, pred[1024]{0:T(1024)(128)(4,1)S(1)} %iota_compare_fusion.2), kind=kLoop, calls=%fused_computation.48 | loop fusion | flops 3145728 | bytes 3148800 | tf_op jit(solution)/shard_map/broadcast_in_dim | solution.py:128
  (34 shorter events, 0.1 us)
Async XLA Ops:
  7.2 176.4 %copy-start = (bf16[512,2048]{1,0:T(8,128)(2,1)S(1)}, bf16[512,2048]{1,0:T(8,128)(2,1)}, u32[]{:S(2)}) copy-start(bf16[512,2048]{1,0:T(8,128)(2,1)} %param.18) | copy-start | bytes 6291460
  7.2 39.6 %all-gather.10.cloned.1.call-start = ((), (), s32[]{:S(2)}) async-start(), calls=%async_computation.4 | async-start | bytes 5242880 | tf_op jit(solution)/shard_map/all_gather | solution.py:28
  7.9 92.0 %all-gather.6.cloned.1.call-start = ((), (), s32[]{:S(2)}) async-start(), calls=%async_computation.1 | async-start | bytes 2359296 | tf_op jit(solution)/shard_map/all_gather | solution.py:54
  9.8 141.5 %all-gather.8.cloned.1.call-start = ((), (), s32[]{:S(2)}) async-start(), calls=%async_computation.2 | async-start | bytes 2359296 | tf_op jit(solution)/shard_map/all_gather | solution.py:55
  11.6 220.5 %reduce-scatter.2.cloned.1.call-start = ((), (), s32[]{:S(2)}) async-start(), calls=%async_computation.3 | async-start | bytes 5242880 | tf_op jit(solution)/shard_map/reduce_scatter | solution.py:122
  40.2 13.0 %copy-start.15 = (f32[3,512]{1,0:T(4,128)S(1)}, f32[3,512]{1,0:T(4,128)}, u32[]{:S(2)}) copy-start(f32[3,512]{1,0:T(4,128)} %param.17) | copy-start | bytes 18436
  40.2 13.0 %copy-start.16 = (f32[2048]{0:T(1024)S(1)}, f32[2048]{0:T(1024)}, u32[]{:S(2)}) copy-start(f32[2048]{0:T(1024)} %param.15) | copy-start | bytes 24580
  40.2 13.0 %copy-start.17 = (f32[2048]{0:T(1024)S(1)}, f32[2048]{0:T(1024)}, u32[]{:S(2)}) copy-start(f32[2048]{0:T(1024)} %param.14) | copy-start | bytes 24580
  46.8 6.4 %copy-start.1 = (bf16[1,1024,2048]{2,1,0:T(8,128)(2,1)S(1)}, bf16[1,1024,2048]{2,1,0:T(8,128)(2,1)}, u32[]{:S(2)}) copy-start(bf16[1,1024,2048]{2,1,0:T(8,128)(2,1)} %all-gather.10.cloned.1.call-done) | copy-start | bytes 12582916
  64.5 35.4 %copy-start.14 = (f32[4]{0:T(128)S(1)}, f32[4]{0:T(128)}, u32[]{:S(2)}) copy-start(f32[4]{0:T(128)} %param.20) | copy-start | bytes 52
  117.8 4.6 %copy-start.3 = (f32[512,1024]{1,0:T(8,128)S(1)}, f32[512,1024]{1,0:T(8,128)}, u32[]{:S(2)}) copy-start(f32[512,1024]{1,0:T(8,128)} %get-tuple-element.34) | copy-start | bytes 6291460
  117.8 4.6 %copy-start.6 = (pred[512,1024]{1,0:T(8,128)(4,1)S(1)}, pred[512,1024]{1,0:T(8,128)(4,1)}, u32[]{:S(2)}) copy-start(pred[512,1024]{1,0:T(8,128)(4,1)} %get-tuple-element.27) | copy-start | bytes 1572868
  117.8 4.6 %copy-start.7 = (f32[512,1024]{1,0:T(8,128)S(1)}, f32[512,1024]{1,0:T(8,128)}, u32[]{:S(2)}) copy-start(f32[512,1024]{1,0:T(8,128)} %get-tuple-element.35) | copy-start | bytes 6291460
  117.8 4.6 %copy-start.10 = (bf16[1,1024,512]{1,2,0:T(8,128)(2,1)S(1)}, bf16[1,1024,512]{1,2,0:T(8,128)(2,1)}, u32[]{:S(2)}) copy-start(bf16[1,1024,512]{1,2,0:T(8,128)(2,1)} %get-tuple-element.21) | copy-start | bytes 3145732
  117.8 4.6 %copy-start.11 = (pred[512,1024]{1,0:T(8,128)(4,1)S(1)}, pred[512,1024]{1,0:T(8,128)(4,1)}, u32[]{:S(2)}) copy-start(pred[512,1024]{1,0:T(8,128)(4,1)} %get-tuple-element.28) | copy-start | bytes 1572868
  117.8 4.6 %copy-start.13 = (bf16[1,512,512]{1,2,0:T(8,128)(2,1)S(1)}, bf16[1,512,512]{1,2,0:T(8,128)(2,1)}, u32[]{:S(2)}) copy-start(bf16[1,512,512]{1,2,0:T(8,128)(2,1)} %get-tuple-element.24) | copy-start | bytes 1572868
  122.4 7.9 %copy-start.18 = (f32[4,512,1024]{2,1,0:T(8,128)}, f32[4,512,1024]{2,1,0:T(8,128)S(1)}, u32[]{:S(2)}) copy-start(f32[4,512,1024]{2,1,0:T(8,128)S(1)} %get-tuple-element.30) | copy-start | bytes 25165828
  151.3 15.1 %copy-start.4 = (f32[512,1024]{1,0:T(8,128)S(1)}, f32[512,1024]{1,0:T(8,128)}, u32[]{:S(2)}) copy-start(f32[512,1024]{1,0:T(8,128)} %get-tuple-element.34) | copy-start | bytes 6291460
  166.3 6.1 %copy-start.2 = (f32[4,512,1024]{2,1,0:T(8,128)S(1)}, f32[4,512,1024]{2,1,0:T(8,128)}, u32[]{:S(2)}) copy-start(f32[4,512,1024]{2,1,0:T(8,128)} %get-tuple-element.33) | copy-start | bytes 25165828
  166.4 6.1 %copy-start.9 = (bf16[1,1024,512]{1,2,0:T(8,128)(2,1)S(1)}, bf16[1,1024,512]{1,2,0:T(8,128)(2,1)}, u32[]{:S(2)}) copy-start(bf16[1,1024,512]{1,2,0:T(8,128)(2,1)} %get-tuple-element.20) | copy-start | bytes 3145732
  166.4 12.0 %slice-start = ((s8[8388608]{0:T(1024)(128)(4,1)}), s8[4194304]{0:T(1024)(128)(4,1)S(1)}, s32[]{:S(2)}) async-start(s8[8388608]{0:T(1024)(128)(4,1)} %bitcast.74), calls=%async_computation.5 | async-start | bytes 8388608
  172.4 5.9 %copy-start.8 = (f32[512,1024]{1,0:T(8,128)S(1)}, f32[512,1024]{1,0:T(8,128)}, u32[]{:S(2)}) copy-start(f32[512,1024]{1,0:T(8,128)} %get-tuple-element.35) | copy-start | bytes 6291460
  172.5 5.9 %copy-start.12 = (pred[512,1024]{1,0:T(8,128)(4,1)S(1)}, pred[512,1024]{1,0:T(8,128)(4,1)}, u32[]{:S(2)}) copy-start(pred[512,1024]{1,0:T(8,128)(4,1)} %get-tuple-element.28) | copy-start | bytes 1572868
  172.5 5.9 %slice-start.1 = ((s8[8388608]{0:T(1024)(128)(4,1)}), s8[4194304]{0:T(1024)(128)(4,1)S(1)}, s32[]{:S(2)}) async-start(s8[8388608]{0:T(1024)(128)(4,1)} %bitcast.74), calls=%async_computation.6 | async-start | bytes 8388608
  172.5 5.9 %copy-start.19 = (f32[4,1024,128]{2,1,0:T(8,128)S(1)}, f32[4,1024,128]{2,1,0:T(8,128)}, u32[]{:S(2)}) copy-start(f32[4,1024,128]{2,1,0:T(8,128)} %fusion.2) | copy-start | bytes 6291460
  183.5 48.6 %copy-start.5 = (bf16[1,1024,512]{2,1,0:T(8,128)(2,1)S(1)}, bf16[1,1024,512]{2,1,0:T(8,128)(2,1)}, u32[]{:S(2)}) copy-start(bf16[1,1024,512]{2,1,0:T(8,128)(2,1)} %param.13) | copy-start | bytes 3145732
Sparse Core Ops, SparseCore 0:
  9.6 37.1 all-gather.9
  48.8 51.0 all-gather.5
  102.0 49.2 all-gather.7
  189.3 42.6 reduce-scatter.1
where the time goes:
time: 242 us; the launch traced here: 241 us
  waiting for transfers between devices  79.7 us (33%)
  matrix products  71.7 us (30%)
  other arithmetic  39.6 us (16%)
  blocking collectives  22.2 us (9%)
  between operations  16.1 us (7%)
  local copies, waits for them, and re-layouts  11.6 us (5%)
    reduce_scatter x1, waiting for transfers between devices, on_device(): lax.psum_scatter(partial_value.astype(jnp.bfloat16), 'tp', scatter_dimens...  37.3 us
    all_gather x1, waiting for transfers between devices, on_device(): key_piece = lax.all_gather(prefix_k, 'req', axis=0, tiled=True)  32.2 us
    all_gather x1, blocking collectives, on_device(): number_piece = lax.all_gather(block_numbers, 'req', axis=0, tiled=True)  22.2 us
    dot_general x1, matrix products, on_device(): jnp.einsum('shd,khd->hsk', query_heads, compute_key_heads, preferred_elem...  17.8 us
    dot_general x1, matrix products, on_device(): jnp.einsum('hsk,khd->hsd', compute_weights.astype(jnp.bfloat16), compute_...  15.1 us
    reduce_sum x1, other arithmetic, on_device(): compute_new_sum = jnp.sum(compute_weights, axis=2)  14.3 us
    dot_general x2, matrix products, on_device(): jnp.einsum('shd,khd->hsk', query_block, key_heads, preferred_element_type...  12.3 us
    dot_general x1, matrix products, on_device(): jnp.einsum('sd,cdh->csh', normed, w_qkv, preferred_element_type=jnp.float32)  11.3 us
  transfers between devices with their start and end apart: 4, of which 4 were waited for; matrix products, arithmetic and copies ran while one was open for 34% of the time, Pallas kernels for 0%

commit v1 on v0

v1 whole, which is shorter than its diff:
```python
import functools
import math

import jax
import jax.numpy as jnp
from jax import lax
from jax.experimental import pallas as pl
from jax.experimental.pallas import tpu as pltpu
from jax.sharding import PartitionSpec as P

EPS = 1e-05
NEGATIVE = -1e30
LOG2E = math.log2(math.e)
ROWS = 256
F32 = jnp.float32
BF16 = jnp.bfloat16


def dot_t(a, b):
    return lax.dot_general(a, b, (((1,), (1,)), ((), ())), preferred_element_type=F32)


def kernel(
    n_req,
    n_x,
    order,
    length_ref,
    slope,
    hid,
    gain,
    beta,
    w_qkv,
    b_qkv,
    w_out,
    b_out,
    pk,
    pv,
    mixed,
    ck,
    cv,
    hbuf,
    wq,
    wo,
    nrm,
    qkv,
    cst,
    kv,
    acc,
    mst,
    lst,
    att,
    pbuf,
    sibr,
    ys,
    yr,
    ost,
    loc_sem,
    out_sem,
    hs,
    hr,
    zs,
    xs,
    kvr,
    ss,
    sr,
    yss,
    yrs,
):
    slots, width = hid.shape[1], hid.shape[2]
    block = pk.shape[0]
    heads, size = qkv.shape[1], qkv.shape[3]
    n_rc = slots // ROWS
    n_z = n_req // n_x
    nb = n_req // 2
    prefix = nb * block
    feats = 4 * width

    r = lax.axis_index("req")
    t = lax.axis_index("tp")
    y, c = t // 2, t % 2
    sib = y * 2 + (1 - c)
    oth = (1 - y) * 2 + c
    far = (1 - y) * 2 + (1 - c)
    z, x = r // n_x, r % n_x
    x_peers = [z * n_x + (x + d) % n_x for d in range(1, n_x)]

    def remote(src, dst, send, recv, dev):
        return pltpu.make_async_remote_copy(
            src_ref=src,
            dst_ref=dst,
            send_sem=send,
            recv_sem=recv,
            device_id=dev,
            device_id_type=pl.DeviceIdType.MESH,
        )

    barrier = pltpu.get_barrier_semaphore()

    def greet(dev):
        pl.semaphore_signal(
            barrier, inc=1, device_id=dev, device_id_type=pl.DeviceIdType.MESH
        )

    greet((r, sib))
    greet((r, oth))
    for peer in x_peers:
        greet((peer, t))

    @pl.when(z > 0)
    def _():
        greet((r - n_x, t))

    @pl.when(z < n_z - 1)
    def _():
        greet((r + n_x, t))

    below, above = (z + n_z - 1) // n_z, (2 * n_z - 2 - z) // n_z
    pl.semaphore_wait(barrier, 2 + len(x_peers) + below + above)

    def rows_of(i):
        return pl.ds(pl.multiple_of(i * ROWS, ROWS), ROWS)

    def h_other(i):
        rows = rows_of(i)
        return remote(
            hid.at[0, rows], hbuf.at[t, rows], hs.at[0, i], hr.at[0, i], (r, oth)
        )

    def h_sib(i):
        rows = rows_of(i)
        return remote(
            hid.at[0, rows], hbuf.at[t, rows], hs.at[1, i], hr.at[1, i], (r, sib)
        )

    def h_fwd(i):
        rows = rows_of(i)
        return remote(
            hbuf.at[oth, rows], hbuf.at[oth, rows], hs.at[2, i], hr.at[2, i], (r, sib)
        )

    def up(src, a, zj):
        return remote(
            src, kv.at[a, zj * n_x + x], zs.at[0, a, zj], kvr.at[a, zj * n_x + x], (r + n_x, t)
        )

    def down(src, a, zj):
        return remote(
            src, kv.at[a, zj * n_x + x], zs.at[1, a, zj], kvr.at[a, zj * n_x + x], (r - n_x, t)
        )

    def across(src, a, zj, d):
        return remote(
            src,
            kv.at[a, zj * n_x + x],
            xs.at[d, a, zj],
            kvr.at[a, zj * n_x + x],
            (x_peers[d], t),
        )

    def kv_wait(a, j):
        remote(kv.at[a, j], kv.at[a, j], hs.at[0, 0], kvr.at[a, j], (r, sib)).wait_recv()

    for i in range(n_rc):
        h_other(i).start()
        h_sib(i).start()
    own = [pltpu.make_async_copy(hid.at[0], hbuf.at[t], loc_sem.at[0])]
    own.append(pltpu.make_async_copy(w_qkv, wq, loc_sem.at[1]))
    own.append(pltpu.make_async_copy(w_out, wo, loc_sem.at[2]))
    own.append(pltpu.make_async_copy(pk, kv.at[0, r], loc_sem.at[3]))
    own.append(pltpu.make_async_copy(pv, kv.at[1, r], loc_sem.at[4]))
    for a, src in ((0, pk), (1, pv)):

        @pl.when(z < n_z - 1)
        def _(a=a, src=src):
            up(src, a, z).start()

        @pl.when(z > 0)
        def _(a=a, src=src):
            down(src, a, z).start()

        for d in range(n_x - 1):
            across(src, a, z, d).start()
    for copy in own:
        copy.start()

    n_events = 2 * (n_z - 1)

    def handle(e):
        s, a = e // 2 + 1, e % 2

        @pl.when(z - s >= 0)
        def _():
            zj = z - s
            here = kv.at[a, zj * n_x + x]
            kv_wait(a, zj * n_x + x)

            @pl.when(z < n_z - 1)
            def _():
                up(here, a, zj).start()

            for d in range(n_x - 1):
                across(here, a, zj, d).start()

        @pl.when(z + s < n_z)
        def _():
            zj = z + s
            here = kv.at[a, zj * n_x + x]
            kv_wait(a, zj * n_x + x)

            @pl.when(z > 0)
            def _():
                down(here, a, zj).start()

            for d in range(n_x - 1):
                across(here, a, zj, d).start()

    length = length_ref[0]

    def live(i):
        ids = lax.broadcasted_iota(jnp.int32, (ROWS, width), 0) + i * ROWS
        return ids < length

    def cache_out(i, j):
        rows = rows_of(i)
        dst = (ck, cv)[j]
        return pltpu.make_async_copy(cst.at[j, rows], dst.at[0, rows], out_sem.at[j, i])

    own[0].wait()
    own[1].wait()

    def project(i, carry):
        rows = rows_of(i)
        h_other(i).wait_recv()
        h_fwd(i).start()
        h_sib(i).wait_recv()
        h_fwd(i).wait_recv()
        pieces = [hbuf[f, rows, :].astype(F32) for f in range(4)]
        mean = sum(jnp.sum(p, axis=1, keepdims=True) for p in pieces) * (1.0 / feats)
        pieces = [p - mean for p in pieces]
        var = sum(jnp.sum(p * p, axis=1, keepdims=True) for p in pieces) * (1.0 / feats)
        inv = 1.0 / jnp.sqrt(var + EPS)
        for f in range(4):
            cols = slice(f * width, (f + 1) * width)
            nrm[:, cols] = (pieces[f] * inv * gain[:, cols] + beta[:, cols]).astype(BF16)
        keep = live(i)
        for j in range(3):
            out = jnp.dot(nrm[...], wq[j], preferred_element_type=F32) + b_qkv[j : j + 1, :]
            out = out.astype(BF16)
            for h in range(heads):
                qkv[j, h, rows, :] = out[:, h * size : (h + 1) * size]
            if j > 0:
                cst[j - 1, rows, :] = jnp.where(keep, out, jnp.zeros_like(out))
                cache_out(i, j - 1).start()

        @pl.when(i < n_events)
        def _():
            handle(i)

        return carry

    lax.fori_loop(0, n_rc, project, 0)

    scale2 = LOG2E / math.sqrt(size)
    tri = lax.broadcasted_iota(jnp.int32, (ROWS, ROWS), 1) <= lax.broadcasted_iota(
        jnp.int32, (ROWS, ROWS), 0
    )

    def suffix(h, carry):
        slope2 = slope[h] * LOG2E
        ids = lax.broadcasted_iota(jnp.int32, (1, slots), 1)
        shift = jnp.where(ids < length, ids.astype(F32) * slope2, NEGATIVE)
        for i in range(n_rc):
            lo, hi = i * ROWS, (i + 1) * ROWS
            q = qkv[0, h, lo:hi, :]
            sd = dot_t(q, qkv[1, h, lo:hi, :]) * scale2 + shift[:, lo:hi]
            sd = jnp.where(tri, sd, NEGATIVE)
            m = jnp.max(sd, axis=1, keepdims=True)
            if i > 0:
                so = dot_t(q, qkv[1, h, 0:lo, :]) * scale2 + shift[:, 0:lo]
                m = jnp.maximum(m, jnp.max(so, axis=1, keepdims=True))
            wd = jnp.exp2(sd - m)
            total = jnp.sum(wd, axis=1, keepdims=True)
            out = jnp.dot(
                wd.astype(BF16), qkv[2, h, lo:hi, :], preferred_element_type=F32
            )
            if i > 0:
                wo_ = jnp.exp2(so - m)
                total = total + jnp.sum(wo_, axis=1, keepdims=True)
                out = out + jnp.dot(
                    wo_.astype(BF16), qkv[2, h, 0:lo, :], preferred_element_type=F32
                )
            acc[h, lo:hi, :] = out
            mst[h, lo:hi, :] = jnp.broadcast_to(m, (ROWS, size))
            lst[h, lo:hi, :] = jnp.broadcast_to(total, (ROWS, size))

        @pl.when(n_rc + h < n_events)
        def _():
            handle(n_rc + h)

        return carry

    lax.fori_loop(0, heads, suffix, 0)

    def late(e, carry):
        handle(e)
        return carry

    if n_events > n_rc + heads:
        lax.fori_loop(n_rc + heads, n_events, late, 0)

    for copy in own[2:]:
        copy.wait()

    def wait_across(zj, carry):
        for a in range(2):
            for d in range(1, n_x):
                kv_wait(a, zj * n_x + (x + d) % n_x)
        return carry

    lax.fori_loop(0, n_z, wait_across, 0)

    def to_sib(i):
        return remote(pbuf.at[i, 1 - c], sibr.at[i], ss.at[i], sr.at[i], (r, sib))

    def to_oth(i):
        return remote(ys.at[i], yr.at[i], yss.at[i], yrs.at[i], (r, oth))

    step = min(4, nb)

    def finish(i, carry):
        rows = rows_of(i)
        for h in range(heads):
            slope2 = slope[h] * LOG2E
            cols = slice(h * size, (h + 1) * size)
            q = qkv[0, h, rows, :]
            m = mst[h, rows, :][:, :1]
            total = lst[h, rows, :][:, :1]
            out = acc[h, rows, :]
            for b0 in range(0, nb, step):
                holders = [order[b] for b in range(b0, b0 + step)]
                keys = jnp.concatenate([kv[0, j, :, cols] for j in holders], axis=0)
                vals = jnp.concatenate([kv[1, j, :, cols] for j in holders], axis=0)
                ids = lax.broadcasted_iota(jnp.int32, (1, step * block), 1)
                shift = (ids + (b0 * block - prefix)).astype(F32) * slope2
                sc = dot_t(q, keys) * scale2 + shift
                new = jnp.maximum(m, jnp.max(sc, axis=1, keepdims=True))
                fac = jnp.exp2(m - new)
                w = jnp.exp2(sc - new)
                total = total * fac + jnp.sum(w, axis=1, keepdims=True)
                out = out * fac + jnp.dot(w.astype(BF16), vals, preferred_element_type=F32)
                m = new
            att[:, cols] = (out / total).astype(BF16)
        for f in range(4):
            part = jnp.dot(
                att[...], wo[:, f * width : (f + 1) * width], preferred_element_type=F32
            )
            pbuf[i, f % 2, f // 2] = part.astype(BF16)
        to_sib(i).start()
        to_sib(i).wait_recv()
        ys[i] = (pbuf[i, c, 1 - y].astype(F32) + sibr[i, 1 - y].astype(F32)).astype(BF16)
        to_oth(i).start()
        return carry

    lax.fori_loop(0, n_rc, finish, 0)

    def mixed_out(i):
        rows = rows_of(i)
        return pltpu.make_async_copy(ost.at[rows], mixed.at[0, rows], out_sem.at[2, i])

    def final(i, carry):
        rows = rows_of(i)
        to_oth(i).wait_recv()
        out = pbuf[i, c, y].astype(F32) + sibr[i, y].astype(F32) + yr[i].astype(F32)
        out = out + b_out[t] + hbuf[t, rows, :].astype(F32)
        ost[rows, :] = jnp.where(live(i), out, 0.0).astype(BF16)
        mixed_out(i).start()
        return carry

    lax.fori_loop(0, n_rc, final, 0)

    def drain(i, carry):
        h_other(i).wait_send()
        h_sib(i).wait_send()
        h_fwd(i).wait_send()
        to_sib(i).wait_send()
        to_oth(i).wait_send()
        cache_out(i, 0).wait()
        cache_out(i, 1).wait()
        mixed_out(i).wait()
        return carry

    lax.fori_loop(0, n_rc, drain, 0)

    def drain_prefix(zj, carry):
        for a in range(2):
            here = kv.at[a, zj * n_x + x]

            @pl.when(jnp.logical_and(zj <= z, z < n_z - 1))
            def _():
                up(here, a, zj).wait_send()

            @pl.when(jnp.logical_and(zj >= z, z > 0))
            def _():
                down(here, a, zj).wait_send()

            for d in range(n_x - 1):
                across(here, a, zj, d).wait_send()
        return carry

    lax.fori_loop(0, n_z, drain_prefix, 0)


def on_device(
    n_req,
    n_x,
    hidden_in,
    ln_gain,
    ln_bias,
    w_qkv,
    b_qkv,
    w_out,
    b_out,
    alibi_slope,
    prefix_k,
    prefix_v,
    suffix_len,
    group_of,
    block_of_device,
):
    _, slots, width = hidden_in.shape
    heads = alibi_slope.shape[0]
    size = w_qkv.shape[2] // heads
    block = prefix_k.shape[0]
    nb = n_req // 2
    n_rc = slots // ROWS
    n_z = n_req // n_x
    numbers = lax.all_gather(block_of_device, "req", axis=0, tiled=True)
    wanted = group_of[0] * nb + lax.iota(jnp.int32, nb)
    match = numbers[None, :] == wanted[:, None]
    order = jnp.sum(jnp.where(match, lax.iota(jnp.int32, n_req)[None, :], 0), axis=1)
    smem = pl.BlockSpec(memory_space=pltpu.SMEM)
    vmem = pl.BlockSpec(memory_space=pltpu.VMEM)
    hbm = pl.BlockSpec(memory_space=pl.ANY)
    dma = pltpu.SemaphoreType.DMA
    cache = jax.ShapeDtypeStruct((1, slots, width), BF16)
    return pl.pallas_call(
        functools.partial(kernel, n_req, n_x),
        out_shape=(cache, cache, cache),
        in_specs=[smem, smem, smem, hbm, vmem, vmem, hbm, vmem, hbm, vmem, hbm, hbm],
        out_specs=(hbm, hbm, hbm),
        scratch_shapes=[
            pltpu.VMEM((4, slots, width), BF16),
            pltpu.VMEM(w_qkv.shape, BF16),
            pltpu.VMEM(w_out.shape, BF16),
            pltpu.VMEM((ROWS, 4 * width), BF16),
            pltpu.VMEM((3, heads, slots, size), BF16),
            pltpu.VMEM((2, slots, width), BF16),
            pltpu.VMEM((2, n_req, block, heads * size), BF16),
            pltpu.VMEM((heads, slots, size), F32),
            pltpu.VMEM((heads, slots, size), F32),
            pltpu.VMEM((heads, slots, size), F32),
            pltpu.VMEM((ROWS, heads * size), BF16),
            pltpu.VMEM((n_rc, 2, 2, ROWS, width), BF16),
            pltpu.VMEM((n_rc, 2, ROWS, width), BF16),
            pltpu.VMEM((n_rc, ROWS, width), BF16),
            pltpu.VMEM((n_rc, ROWS, width), BF16),
            pltpu.VMEM((slots, width), BF16),
            dma((5,)),
            dma((3, n_rc)),
            dma((3, n_rc)),
            dma((3, n_rc)),
            dma((2, 2, n_z)),
            dma((n_x - 1, 2, n_z)),
            dma((2, n_req)),
            dma((n_rc,)),
            dma((n_rc,)),
            dma((n_rc,)),
            dma((n_rc,)),
        ],
        compiler_params=pltpu.CompilerParams(
            collective_id=0, has_side_effects=True, vmem_limit_bytes=60 << 20
        ),
        name="sublayer",
    )(
        order,
        suffix_len,
        alibi_slope,
        hidden_in,
        ln_gain[None],
        ln_bias[None],
        w_qkv,
        b_qkv,
        w_out,
        b_out.reshape(4, 1, width),
        prefix_k,
        prefix_v,
    )


def solution(mesh):
    n_req = mesh.shape["req"]
    n_x = 2 if n_req <= 8 else 4
    return jax.shard_map(
        functools.partial(on_device, n_req, n_x),
        mesh=mesh,
        in_specs=(
            P("req", None, "tp"),
            P(),
            P(),
            P(None, None, "tp"),
            P(None, "tp"),
            P("tp", None),
            P(),
            P("tp"),
            P("req", "tp"),
            P("req", "tp"),
            P("req"),
            P("req"),
            P("req"),
        ),
        out_specs=(P("req", None, "tp"), P("req", None, "tp"), P("req", None, "tp")),
        check_vma=False,
    )
```

time: 242 us -> 106 us (0.44)
  Pallas kernels: 0 us -> 80.4 us
  waiting for transfers between devices: 79.7 us -> 0 us
  matrix products: 71.7 us -> 0 us
  other arithmetic: 39.6 us -> 0.7 us
  between operations: 16.1 us -> 2.59 us
  blocking collectives: 22.2 us -> 13.1 us
  local copies, waits for them, and re-layouts: 11.6 us -> 8.78 us
    pallas_call x0 -> x1, Pallas kernels: none -> 80.4 us  [on_device(): pl.pallas_call(functools.partial(kernel, n_req, n_x), out_shape=(cache, c...]
    dot_general x8 -> x0, matrix products: 71.7 us -> none  [the longest x1 17.8 us: on_device(): jnp.einsum('shd,khd->hsk', query_heads, compute_key_heads, preferred_elem...]
    all_gather x3 -> x0, waiting for transfers between devices: 41.7 us -> none  [the longest x1 32.2 us: on_device(): key_piece = lax.all_gather(prefix_k, 'req', axis=0, tiled=True)]
    reduce_scatter x1 -> x0, waiting for transfers between devices: 37.3 us -> none  [on_device(): lax.psum_scatter(partial_value.astype(jnp.bfloat16), 'tp', scatter_dimens...]
    reduce_sum x4 -> x1, other arithmetic: 26.7 us -> 0.69 us  [on_device(): jnp.sum(jnp.where(match, lax.iota(jnp.int32, n_req)[None, :], 0), axis=1)]
    all_gather x1 -> x0, blocking collectives: 22.2 us -> none  [on_device(): number_piece = lax.all_gather(block_numbers, 'req', axis=0, tiled=True)]
    unnamed x0 -> x1, blocking collectives: none -> 13.1 us
    sub x1 -> x0, other arithmetic: 3.83 us -> none  [on_device(): query_pos[None, :, None] - key_pos[None, None, :]]
  transfers between devices with their start and end apart: 4 -> 0, of which waited for: 4 -> 0; matrix products, arithmetic and copies ran while one was open for 34% -> 0% of each run, Pallas kernels for 0% -> 0%
where the time goes in v1:
time: 106 us
  Pallas kernels  80.4 us (76%)
  blocking collectives  13.1 us (12%)
  local copies, waits for them, and re-layouts  8.78 us (8%)
  between operations  2.59 us (2%)
    pallas_call x1, Pallas kernels, on_device(): pl.pallas_call(functools.partial(kernel, n_req, n_x), out_shape=(cache, c...  80.4 us
    unnamed x1, blocking collectives  13.1 us
    unnamed x6, local copies, waits for them, and re-layouts  8.78 us

profile of v1, /device:TPU:0, one launch (start us, length us, event | category | flops | bytes accessed | tf_op | source)
XLA Modules:
  0.0 105.5 jit_solution(6118154666333503376)
XLA Ops:
  2.6 1.2 %dynamic-slice = u32[1]{0:T(128)} dynamic-slice(u32[32]{0:T(128)} %constant.11, u32[]{:T(128)S(6)} %add.12), dynamic_slice_sizes={1} | dynamic-slice | bytes 12
  3.8 0.8 dynamic-update-slice
  4.6 13.1 %all-reduce = s32[8]{0:T(128)S(1)} all-reduce(s32[8]{0:T(128)S(1)} %dynamic-update-slice), channel_id=1, replica_groups=mesh['req'=8,'tp'=4] {'req'}, use_global_device_ids=true, to_apply=%add | all-reduce | flops 8 | bytes 64
  17.6 0.7 select_reduce_fusion.order
  18.3 80.4 %sublayer.1 = (bf16[1,1024,512]{2,1,0:T(8,128)(2,1)}, bf16[1,1024,512]{2,1,0:T(8,128)(2,1)}, bf16[1,1024,512]{2,1,0:T(8,128)(2,1)}) custom-call(s32[4]{0:T(128)} %select_reduce_fusion.order, s32[1]{0:T(128)S(6)} %copy.20.length_ref, f32[4]{0:T(128)} %slope.1, bf16[1,1024,512]{2,1,0:T(8,128)(2,1)} %hid.1, f32[1,2048]{1,0:T(1,128)} %bitcast.5, ...), custom_call_target="tpu_custom_call" | custom-call | tf_op jit(solution)/shard_map/sublayer/pallas_call | solution.py:446
  98.8 2.3 %copy.23 = bf16[1,1024,512]{2,1,0:T(8,128)(2,1)} copy(bf16[1,1024,512]{2,1,0:T(8,128)(2,1)} %get-tuple-element.6) | data formatting | bytes 2097152
  101.0 2.3 %copy.24 = bf16[1,1024,512]{2,1,0:T(8,128)(2,1)} copy(bf16[1,1024,512]{2,1,0:T(8,128)(2,1)} %get-tuple-element.7) | data formatting | bytes 2097152
  103.3 2.3 %copy.25 = bf16[1,1024,512]{2,1,0:T(8,128)(2,1)} copy(bf16[1,1024,512]{2,1,0:T(8,128)(2,1)} %get-tuple-element.8) | data formatting | bytes 2097152
  (2 shorter events, 0.0 us)

commit v2 on v1

--- a/solution.py
+++ b/solution.py
@@ -23,7 +23,8 @@
 def kernel(
     n_req,
     n_x,
-    order,
+    block_ref,
+    group_ref,
     length_ref,
     slope,
     hid,
@@ -54,6 +55,8 @@
     ys,
     yr,
     ost,
+    ids,
+    mine,
     loc_sem,
     out_sem,
     hs,
@@ -65,6 +68,8 @@
     sr,
     yss,
     yrs,
+    ids_send,
+    ids_recv,
 ):
     slots, width = hid.shape[1], hid.shape[2]
     block = pk.shape[0]
@@ -103,19 +108,27 @@
 
     greet((r, sib))
     greet((r, oth))
-    for peer in x_peers:
-        greet((peer, t))
-
-    @pl.when(z > 0)
-    def _():
-        greet((r - n_x, t))
-
-    @pl.when(z < n_z - 1)
-    def _():
-        greet((r + n_x, t))
-
-    below, above = (z + n_z - 1) // n_z, (2 * n_z - 2 - z) // n_z
-    pl.semaphore_wait(barrier, 2 + len(x_peers) + below + above)
+
+    def greet_req(d, carry):
+        greet(((r + d) % n_req, t))
+        return carry
+
+    lax.fori_loop(1, n_req, greet_req, 0)
+    pl.semaphore_wait(barrier, n_req + 1)
+
+    def number(d):
+        return remote(
+            mine, ids.at[r], ids_send.at[d], ids_recv.at[r], ((r + d) % n_req, t)
+        )
+
+    mine[...] = jnp.full(mine.shape, block_ref[0], jnp.int32)
+    ids[r] = jnp.full(mine.shape, block_ref[0], jnp.int32)
+
+    def send_number(d, carry):
+        number(d).start()
+        return carry
+
+    lax.fori_loop(1, n_req, send_number, 0)
 
     def rows_of(i):
         return pl.ds(pl.multiple_of(i * ROWS, ROWS), ROWS)
@@ -319,13 +332,34 @@
 
     lax.fori_loop(0, n_z, wait_across, 0)
 
+    def wait_number(d, carry):
+        j = (r + d) % n_req
+        remote(ids.at[j], ids.at[j], hs.at[0, 0], ids_recv.at[j], (r, sib)).wait_recv()
+        number(d).wait_send()
+        return carry
+
+    lax.fori_loop(1, n_req, wait_number, 0)
+    first = group_ref[0] * nb
+
     def to_sib(i):
         return remote(pbuf.at[i, 1 - c], sibr.at[i], ss.at[i], sr.at[i], (r, sib))
 
     def to_oth(i):
         return remote(ys.at[i], yr.at[i], yss.at[i], yrs.at[i], (r, oth))
 
-    step = min(4, nb)
+    step = 4
+    inner = lax.broadcasted_iota(jnp.int32, (1, block), 1) - prefix
+
+    def local_number(j):
+        row = ids[j, 0:1, :] - first
+        return jnp.concatenate([row] * (block // row.shape[1]), axis=1)
+
+    def shift_of(j):
+        return (local_number(j) * block + inner).astype(F32)
+
+    def veil_of(j):
+        number = local_number(j)
+        return jnp.where((number >= 0) & (number < nb), 0.0, NEGATIVE)
 
     def finish(i, carry):
         rows = rows_of(i)
@@ -336,19 +370,28 @@
             m = mst[h, rows, :][:, :1]
             total = lst[h, rows, :][:, :1]
             out = acc[h, rows, :]
-            for b0 in range(0, nb, step):
-                holders = [order[b] for b in range(b0, b0 + step)]
+
+            def fold(g, state):
+                m, total, out = state
+                holders = [g * step + k for k in range(step)]
                 keys = jnp.concatenate([kv[0, j, :, cols] for j in holders], axis=0)
                 vals = jnp.concatenate([kv[1, j, :, cols] for j in holders], axis=0)
-                ids = lax.broadcasted_iota(jnp.int32, (1, step * block), 1)
-                shift = (ids + (b0 * block - prefix)).astype(F32) * slope2
-                sc = dot_t(q, keys) * scale2 + shift
+                shift = [shift_of(j) * slope2 + veil_of(j) for j in holders]
+                sc = dot_t(q, keys) * scale2 + jnp.concatenate(shift, axis=1)
                 new = jnp.maximum(m, jnp.max(sc, axis=1, keepdims=True))
                 fac = jnp.exp2(m - new)
                 w = jnp.exp2(sc - new)
                 total = total * fac + jnp.sum(w, axis=1, keepdims=True)
                 out = out * fac + jnp.dot(w.astype(BF16), vals, preferred_element_type=F32)
-                m = new
+                return new, total, out
+
+            state = (m, total, out)
+            if n_req <= 2 * step:
+                for g in range(n_req // step):
+                    state = fold(g, state)
+            else:
+                state = lax.fori_loop(0, n_req // step, fold, state)
+            m, total, out = state
             att[:, cols] = (out / total).astype(BF16)
         for f in range(4):
             part = jnp.dot(
@@ -431,23 +474,19 @@
     heads = alibi_slope.shape[0]
     size = w_qkv.shape[2] // heads
     block = prefix_k.shape[0]
-    nb = n_req // 2
     n_rc = slots // ROWS
     n_z = n_req // n_x
-    numbers = lax.all_gather(block_of_device, "req", axis=0, tiled=True)
-    wanted = group_of[0] * nb + lax.iota(jnp.int32, nb)
-    match = numbers[None, :] == wanted[:, None]
-    order = jnp.sum(jnp.where(match, lax.iota(jnp.int32, n_req)[None, :], 0), axis=1)
     smem = pl.BlockSpec(memory_space=pltpu.SMEM)
     vmem = pl.BlockSpec(memory_space=pltpu.VMEM)
-    hbm = pl.BlockSpec(memory_space=pl.ANY)
+    hbm = pl.BlockSpec(memory_space=pltpu.HBM)
+    anywhere = pl.BlockSpec(memory_space=pl.ANY)
     dma = pltpu.SemaphoreType.DMA
     cache = jax.ShapeDtypeStruct((1, slots, width), BF16)
     return pl.pallas_call(
         functools.partial(kernel, n_req, n_x),
         out_shape=(cache, cache, cache),
-        in_specs=[smem, smem, smem, hbm, vmem, vmem, hbm, vmem, hbm, vmem, hbm, hbm],
-        out_specs=(hbm, hbm, hbm),
+        in_specs=[smem, smem, smem, smem, hbm, vmem, vmem, hbm, vmem, hbm, vmem, hbm, hbm],
+        out_specs=(anywhere, anywhere, anywhere),
         scratch_shapes=[
             pltpu.VMEM((4, slots, width), BF16),
             pltpu.VMEM(w_qkv.shape, BF16),
@@ -465,6 +504,8 @@
             pltpu.VMEM((n_rc, ROWS, width), BF16),
             pltpu.VMEM((n_rc, ROWS, width), BF16),
             pltpu.VMEM((slots, width), BF16),
+            pltpu.VMEM((n_req, 8, 128), jnp.int32),
+            pltpu.VMEM((8, 128), jnp.int32),
             dma((5,)),
             dma((3, n_rc)),
             dma((3, n_rc)),
@@ -476,13 +517,16 @@
             dma((n_rc,)),
             dma((n_rc,)),
             dma((n_rc,)),
+            dma((n_req,)),
+            dma((n_req,)),
         ],
         compiler_params=pltpu.CompilerParams(
-            collective_id=0, has_side_effects=True, vmem_limit_bytes=60 << 20
+            collective_id=0, has_side_effects=True, vmem_limit_bytes=(42 << 20) + 4 * n_req * block * width
         ),
         name="sublayer",
     )(
-        order,
+        block_of_device,
+        group_of,
         suffix_len,
         alibi_slope,
         hidden_in,

time: 106 us -> 105 us (level)
  blocking collectives: 13.1 us -> 0 us
  Pallas kernels: 80.4 us -> 91.1 us
  local copies, waits for them, and re-layouts: 8.78 us -> 11.1 us
    unnamed x1 -> x0, blocking collectives: 13.1 us -> none
    pallas_call x1, Pallas kernels: 80.4 us -> 91.1 us  [on_device(): pl.pallas_call(functools.partial(kernel, n_req, n_x), out_shape=(cache, c...]
    unnamed x6 -> x21, local copies, waits for them, and re-layouts: 8.78 us -> 11.1 us
where the time goes in v2:
time: 105 us
  Pallas kernels  91.1 us (87%)
  local copies, waits for them, and re-layouts  11.1 us (11%)
  between operations  2.6 us (2%)
    pallas_call x1, Pallas kernels, on_device(): pl.pallas_call(functools.partial(kernel, n_req, n_x), out_shape=(cache, c...  91.1 us
    unnamed x21, local copies, waits for them, and re-layouts  11.1 us

profile of v2, /device:TPU:0, one launch (start us, length us, event | category | flops | bytes accessed | tf_op | source)
XLA Modules:
  0.0 104.8 jit_solution(241332192415582704)
XLA Ops:
  2.6 0.0 copy-start
  2.6 1.6 %copy-done = bf16[512,2048]{1,0:T(8,128)(2,1)S(1)} copy-done((bf16[512,2048]{1,0:T(8,128)(2,1)S(1)}, bf16[512,2048]{1,0:T(8,128)(2,1)}, u32[]{:S(2)}) %copy-start) | copy-done | bytes 2097176
  4.2 0.0 copy-start.1
  4.2 1.2 %copy-done.1 = bf16[1,1024,512]{2,1,0:T(8,128)(2,1)S(1)} copy-done((bf16[1,1024,512]{2,1,0:T(8,128)(2,1)S(1)}, bf16[1,1024,512]{2,1,0:T(8,128)(2,1)}, u32[]{:S(2)}) %copy-start.1) | copy-done | bytes 1048600
  5.4 0.0 copy-start.2
  5.4 0.9 copy-done.2
  6.3 0.0 copy-start.3
  6.3 0.9 copy-done.3
  7.3 0.0 copy-start.4
  7.3 0.7 copy-done.4
  8.0 0.0 copy-start.5
  8.0 0.7 copy-done.5
  8.7 0.0 copy-start.6
  8.7 0.7 copy-done.6
  9.4 0.0 copy-start.7
  9.4 0.7 copy-done.7
  10.1 0.0 copy-start.8
  10.1 0.7 copy-done.8
  10.7 91.1 %sublayer.1 = (bf16[1,1024,512]{2,1,0:T(8,128)(2,1)S(1)}, bf16[1,1024,512]{2,1,0:T(8,128)(2,1)S(1)}, bf16[1,1024,512]{2,1,0:T(8,128)(2,1)S(1)}) custom-call(s32[1]{0:T(128)S(6)} %copy.21.block_ref, s32[1]{0:T(128)S(6)} %copy.20.group_ref, s32[1]{0:T(128)S(6)} %copy.19.length_ref, f32[4]{0:T(128)S(1)} %copy-done.8, bf16[1,1024,512]{2,1,0:T(8,128)(2,1)S(1)} %copy-done.1, ...), custom_call_target="tpu_custom_call" | custom-call | tf_op jit(solution)/shard_map/sublayer/pallas_call | solution.py:485
  101.8 1.0 copy.22
  102.8 1.0 copy.23
  103.8 1.0 copy.24
Async XLA Ops:
  2.6 1.6 %copy-start = (bf16[512,2048]{1,0:T(8,128)(2,1)S(1)}, bf16[512,2048]{1,0:T(8,128)(2,1)}, u32[]{:S(2)}) copy-start(bf16[512,2048]{1,0:T(8,128)(2,1)} %w_out.1) | copy-start | bytes 6291460
  4.2 1.2 %copy-start.1 = (bf16[1,1024,512]{2,1,0:T(8,128)(2,1)S(1)}, bf16[1,1024,512]{2,1,0:T(8,128)(2,1)}, u32[]{:S(2)}) copy-start(bf16[1,1024,512]{2,1,0:T(8,128)(2,1)} %hid.1) | copy-start | bytes 3145732
  5.4 0.9 copy-start.2
  6.3 0.9 copy-start.3
  7.3 0.7 copy-start.4
  8.0 0.7 copy-start.5
  8.7 0.7 copy-start.6
  9.4 0.7 copy-start.7
  10.1 0.7 copy-start.8
